TPU v7x, 32 devices: a whole 2x2x4 slice. The times are simulated.
32 devices in a mesh: grp: 2 (over y), slc: 4 (over z), coil: 2 (over x), vol: 2 (over core).
Axes of the slice: x: 2, y: 2, z: 4, core: 2. Of those that a mesh axis runs over, the one named last changes fastest.
Arguments:
- images: bfloat16 [4, 32, 2, 220, 220], P(('grp', 'vol'), 'slc'), parts along dimension 0, may hold values from -6 to 6
- coil_maps: bfloat16 [8, 32, 2, 220, 220], P(('grp', 'coil'), 'slc'), parts along dimension 0, may hold values from -3 to 3
- kspace: bfloat16 [4, 4, 4, 2, 220, 220], P(('grp', 'vol'), 'slc', 'coil'), parts along dimension 0, may hold values from -12 to 12
- shift_index: int32 [32], P('slc'), may hold values from 0 to 7
- phase_offset: float32 [32, 220], P('slc'), may hold values from -3.140625 to 3.140625
- group_order: int32 [4], replicated, may hold values from 0 to 3, each once
Outputs:
- grad_phase: float32 [64, 220], P(('grp', 'slc')), parts along dimension 0
There are 2 independent parts, one for each index of `grp`. A program takes and returns all parts, laid end to end along the dimension named above; an argument that names none is the same for every part. Nothing has to cross between parts.
Inputs may be any that keep to these rules, and one draw needn't show every extreme that they name: group_order names each of the 4 measured rows exactly once.
All inputs are finite; a program needn't handle non-finite values.
Results may differ from a plain program's by a relative error of at most 0.0096.
Values may be sent and summed in bfloat16 or wider, within the bound.
A program may use at most 64 MiB of HBM per device.

v0:
```python
import functools
import math

import jax
import jax.numpy as jnp
import numpy as np
from jax import lax
from jax.experimental import pallas as pl
from jax.experimental.pallas import tpu as pltpu
from jax.sharding import PartitionSpec as P

MB = 8


def fourier_tables(length):
    positions = jnp.arange(length, dtype=jnp.int32)
    product = positions[:, None] * positions[None, :] % length
    radians = 2.0 * math.pi / length * product.astype(jnp.float32)
    factor = 1.0 / math.sqrt(length)
    return (
        (jnp.cos(radians) * factor).astype(jnp.bfloat16),
        (-jnp.sin(radians) * factor).astype(jnp.bfloat16),
    )


def slice_phases(shift_index, phase_offset, length):
    lines = (jnp.arange(length, dtype=jnp.int32) - length // 2).astype(jnp.float32)
    return (
        2.0 * math.pi / MB * (shift_index.astype(jnp.float32)[:, None] * lines[None, :])
        + phase_offset
    )


ROWS = 32
LAG = 3
MESH = pl.DeviceIdType.MESH
F32 = jnp.float32
BF16 = jnp.bfloat16


def round_up(value, unit):
    return -(-value // unit) * unit


def static_tables(length):
    positions = np.arange(length, dtype=np.int32)
    product = positions[:, None] * positions[None, :] % length
    radians = np.float32(2.0 * math.pi / length) * product.astype(np.float32)
    factor = np.float32(1.0 / math.sqrt(length))
    cosine = (np.cos(radians) * factor).astype(jnp.bfloat16)
    sine = (-np.sin(radians) * factor).astype(jnp.bfloat16)
    return np.asarray(cosine, np.float32), np.asarray(sine, np.float32)


def stage_tables(length, coils):
    cosine, sine = static_tables(length)
    rows, wide = round_up(length, ROWS), round_up(length, 128)
    first = np.zeros((3, rows, length), np.float32)
    first[0, :length], first[1, :length], first[2, :length] = cosine, sine, -sine
    forward = np.zeros((coils, 2, length, coils * 2 * length), np.float32)
    back = np.zeros((coils * 2 * length, coils * 2 * wide), np.float32)
    for coil in range(coils):
        low = coil * 2 * length
        mid, top = low + length, low + 2 * length
        forward[coil, 0, :, low:mid], forward[coil, 0, :, mid:top] = cosine, sine
        forward[coil, 1, :, low:mid], forward[coil, 1, :, mid:top] = -sine, cosine
        at = coil * 2 * wide
        back[low:mid, at : at + length], back[mid:top, at : at + length] = cosine, sine
        at = at + wide
        back[low:mid, at : at + length], back[mid:top, at : at + length] = -sine, cosine
    return first.astype(jnp.bfloat16), forward.astype(jnp.bfloat16), back.astype(jnp.bfloat16)


def kernel(
    sizes,
    order_ref,
    trig_in,
    images_ref,
    maps_ref,
    measured_in,
    first_ref,
    forward_ref,
    back_ref,
    out_ref,
    turned,
    own,
    to_right,
    to_left,
    from_left,
    from_right,
    columns,
    trig_ref,
    measured_ref,
    shares,
    right_send,
    left_send,
    left_recv,
    right_recv,
    share_send,
    share_recv,
):
    groups, coil_axis, vol_axis = sizes
    per_device = images_ref.shape[1]
    length = images_ref.shape[-1]
    coils = maps_ref.shape[0]
    rows, wide = first_ref.shape[1], turned.shape[-1] // (2 * coils)
    spread = per_device // groups
    parts = rows // ROWS
    total = groups * parts
    spot = lax.axis_index("slc")
    coil_at, vol_at = lax.axis_index("coil"), lax.axis_index("vol")
    has_left, has_right = spot > 0, spot < groups - 1
    peers = coil_axis * vol_axis
    mine = coil_at * vol_axis + vol_at

    def peer(distance):
        other = lax.rem(mine + distance, peers)
        return {"coil": other // vol_axis, "vol": lax.rem(other, vol_axis)}

    barrier = pltpu.get_barrier_semaphore()

    @pl.when(has_left)
    def _():
        pl.semaphore_signal(barrier, inc=1, device_id={"slc": spot - 1}, device_id_type=MESH)

    @pl.when(has_right)
    def _():
        pl.semaphore_signal(barrier, inc=1, device_id={"slc": spot + 1}, device_id_type=MESH)

    for distance in range(1, peers):
        pl.semaphore_signal(barrier, inc=1, device_id=peer(distance), device_id_type=MESH)

    def right_copy(chunk):
        return pltpu.make_async_remote_copy(
            src_ref=to_right.at[chunk],
            dst_ref=from_left.at[chunk],
            send_sem=right_send.at[chunk],
            recv_sem=left_recv.at[chunk],
            device_id={"slc": spot + 1},
            device_id_type=MESH,
        )

    def left_copy(chunk):
        return pltpu.make_async_remote_copy(
            src_ref=to_left.at[chunk],
            dst_ref=from_right.at[chunk],
            send_sem=left_send.at[chunk],
            recv_sem=right_recv.at[chunk],
            device_id={"slc": spot - 1},
            device_id_type=MESH,
        )

    turned[...] = jnp.zeros_like(turned)
    columns[...] = jnp.zeros_like(columns)
    trig_ref[...] = jnp.zeros_like(trig_ref)
    measured_ref[...] = jnp.zeros_like(measured_ref)
    trig_ref[:length] = trig_in[...]
    measured_ref[:length] = measured_in[...]

    def dot(left, right):
        return jnp.dot(left, right, preferred_element_type=F32)

    def compute(group):
        sums = [[None, None] for _ in range(coils)]
        for step in range(spread):
            within = group + step * groups
            image_re = images_ref[0, within, 0].astype(F32)
            image_im = images_ref[0, within, 1].astype(F32)
            cosine = trig_ref[:, within : within + 1]
            sine = trig_ref[:, per_device + within : per_device + within + 1]
            for coil in range(coils):
                coil_map = jnp.swapaxes(maps_ref[coil, within].astype(F32), 0, 1)
                map_re, map_im = coil_map[0], coil_map[1]
                coil_re = (map_re * image_re - map_im * image_im).astype(BF16)
                coil_im = (map_re * image_im + map_im * image_re).astype(BF16)
                part_re = dot(first_ref[0], coil_re) + dot(first_ref[2], coil_im)
                part_im = dot(first_ref[0], coil_im) + dot(first_ref[1], coil_re)
                turn_re = part_re * cosine - part_im * sine
                turn_im = part_re * sine + part_im * cosine
                at = coil * 2 * wide
                turned[within, :, at : at + length] = (-turn_im).astype(BF16)
                turned[within, :, at + wide : at + wide + length] = turn_re.astype(BF16)
                for which, value in enumerate((turn_re, turn_im)):
                    before = sums[coil][which]
                    sums[coil][which] = value if before is None else before + value
        spectrum = None
        for coil in range(coils):
            for which in range(2):
                term = dot(sums[coil][which].astype(BF16), forward_ref[coil, which])
                spectrum = term if spectrum is None else spectrum + term
        held = jnp.where(order_ref[group] == spot, F32(1.0), F32(0.0))
        spectrum = spectrum - held * measured_ref[...].astype(F32)
        own[group * parts : (group + 1) * parts] = spectrum.reshape(parts, ROWS, -1)

        @pl.when(jnp.logical_not(has_left))
        def _():
            for chunk in range(group * parts, (group + 1) * parts):
                to_right[chunk] = own[chunk].astype(BF16)
                right_copy(chunk).start()

        @pl.when(jnp.logical_not(has_right))
        def _():
            for chunk in range(group * parts, (group + 1) * parts):
                to_left[chunk] = own[chunk].astype(BF16)
                left_copy(chunk).start()

    between = jnp.where(has_left & has_right, LAG, 0)
    late_right = between * jnp.maximum(0, 2 * spot - (groups - 1))
    late_left = between * jnp.maximum(0, (groups - 1) - 2 * spot)
    extra = LAG * (groups - 3)

    def wave(tick, carry):
        chunk = tick - late_right

        @pl.when(has_left & (chunk >= 0) & (chunk < total))
        def _():
            right_copy(chunk).wait_recv()

            @pl.when(has_right)
            def _():
                to_right[chunk] = (from_left[chunk].astype(F32) + own[chunk]).astype(BF16)
                right_copy(chunk).start()

        other = tick - late_left

        @pl.when(has_right & (other >= 0) & (other < total))
        def _():
            left_copy(other).wait_recv()

            @pl.when(has_left)
            def _():
                to_left[other] = (from_right[other].astype(F32) + own[other]).astype(BF16)
                left_copy(other).start()

        return carry

    def gradient(group):
        span = pl.ds(group * parts, parts)
        value = own[span]
        value = value + jnp.where(has_left, from_left[span].astype(F32), F32(0.0))
        value = value + jnp.where(has_right, from_right[span].astype(F32), F32(0.0))
        value = value.reshape(rows, -1).astype(BF16)
        pulled = dot(value, back_ref[...])
        for step in range(spread):
            within = group + step * groups
            product = pulled * turned[within].astype(F32)
            columns[0:rows, within : within + 1] = jnp.sum(product, axis=1, keepdims=True)

    def ticks(group):
        low = 0 if group == 0 else group * parts + extra
        high = (group + 1) * parts + extra
        end_low = group * parts if group == groups - 1 else 0
        end_high = (group + 1) * parts if group >= groups - 2 else 0
        inner = has_left & has_right
        lax.fori_loop(
            jnp.where(inner, low, end_low), jnp.where(inner, high, end_high), wave, 0
        )

    arrivals = has_left.astype(jnp.int32) + has_right.astype(jnp.int32) + (peers - 1)
    pl.semaphore_wait(barrier, arrivals)
    compute(0)
    for group in range(1, groups):
        compute(group)
        if group < groups - 1:
            ticks(group - 1)
    ticks(groups - 2)
    for group in range(groups - 2):
        gradient(group)
    ticks(groups - 1)
    for group in range(groups - 2, groups):
        gradient(group)

    shares[mine] = columns[...].T[:per_device]

    def share_copy(distance):
        return pltpu.make_async_remote_copy(
            src_ref=shares.at[mine],
            dst_ref=shares.at[mine],
            send_sem=share_send.at[distance],
            recv_sem=share_recv.at[distance],
            device_id=peer(distance),
            device_id_type=MESH,
        )

    for distance in range(1, peers):
        share_copy(distance).start()

    @pl.when(has_right)
    def _():
        def done(chunk, carry):
            right_copy(chunk).wait_send()
            return carry

        lax.fori_loop(0, total, done, 0)

    @pl.when(has_left)
    def _():
        def done(chunk, carry):
            left_copy(chunk).wait_send()
            return carry

        lax.fori_loop(0, total, done, 0)

    for distance in range(1, peers):
        share_copy(distance).wait()
    result = shares[0]
    for other in range(1, peers):
        result = result + shares[other]
    out_ref[...] = result[:, :length] * (1.0 / (coils * peers))


def fused(images, coil_maps, kspace, shift_index, phase_offset, group_order):
    per_device, length = images.shape[1], images.shape[-1]
    coils = coil_maps.shape[0]
    groups = lax.axis_size("slc")
    sizes = (groups, lax.axis_size("coil"), lax.axis_size("vol"))
    peers = sizes[1] * sizes[2]
    first, forward, back = stage_tables(length, coils)
    rows, wide = first.shape[1], back.shape[1] // (2 * coils)
    width = coils * 2 * length
    angle = slice_phases(shift_index, phase_offset, length)
    trig = jnp.concatenate([jnp.cos(angle), jnp.sin(angle)], axis=0)
    trig = trig.T
    measured = jnp.moveaxis(kspace[0, 0], 2, 0).reshape(length, width)
    chunks = groups * rows // ROWS
    vmem = pl.BlockSpec(memory_space=pltpu.VMEM)
    smem = pl.BlockSpec(memory_space=pltpu.SMEM)
    block = pltpu.VMEM((chunks, ROWS, width), BF16)
    side = pltpu.SemaphoreType.DMA((chunks,))
    return pl.pallas_call(
        functools.partial(kernel, sizes),
        out_shape=jax.ShapeDtypeStruct((per_device, length), F32),
        in_specs=[smem] + [vmem] * 7,
        out_specs=vmem,
        scratch_shapes=[
            pltpu.VMEM((per_device, rows, coils * 2 * wide), BF16),
            pltpu.VMEM((chunks, ROWS, width), F32),
            block,
            block,
            block,
            block,
            pltpu.VMEM((wide, 128), F32),
            pltpu.VMEM((rows, 2 * per_device), F32),
            pltpu.VMEM((rows, width), BF16),
            pltpu.VMEM((peers, per_device, wide), F32),
            side,
            side,
            side,
            side,
            pltpu.SemaphoreType.DMA((peers,)),
            pltpu.SemaphoreType.DMA((peers,)),
        ],
        compiler_params=pltpu.CompilerParams(
            collective_id=0, has_side_effects=True, vmem_limit_bytes=60 * 2**20
        ),
    )(
        group_order,
        trig,
        images,
        jnp.swapaxes(coil_maps, 2, 3),
        measured,
        jnp.asarray(first),
        jnp.asarray(forward),
        jnp.asarray(back),
    )


def program(images, coil_maps, kspace, shift_index, phase_offset, group_order):
    arguments = (images, coil_maps, kspace, shift_index, phase_offset, group_order)
    groups = lax.axis_size("slc")
    even = images.shape[1] % groups == 0 and images.shape[0] == 1 and kspace.shape[1] == 1
    if even and images.shape[1] <= 128 and groups > 2:
        return fused(*arguments)
    return body(*arguments)


def body(images, coil_maps, kspace, shift_index, phase_offset, group_order):
    per_device = images.shape[1]
    matrix = images.shape[-1]
    groups = lax.axis_size("slc")
    spread = max(1, per_device // groups)
    slot_count = groups * spread
    cos_table, sin_table = fourier_tables(matrix)
    section_one = jnp.stack([jnp.stack([cos_table, -sin_table]), jnp.stack([sin_table, cos_table])])
    section_two = jnp.stack([jnp.stack([cos_table, sin_table]), jnp.stack([-sin_table, cos_table])])
    image_re = images[:, None, :, 0].astype(jnp.float32)
    image_im = images[:, None, :, 1].astype(jnp.float32)
    map_re = coil_maps[None, :, :, 0].astype(jnp.float32)
    map_im = coil_maps[None, :, :, 1].astype(jnp.float32)
    coil_image = jnp.stack(
        [map_re * image_re - map_im * image_im, map_re * image_im + map_im * image_re], axis=3
    ).astype(jnp.bfloat16)
    partly = jnp.einsum(
        "pqky,tcsqyx->tcspkx", section_one, coil_image, preferred_element_type=jnp.float32
    ).astype(jnp.bfloat16)
    spectra = jnp.einsum(
        "tcsqyx,qpkx->tcspyk", partly, section_two, preferred_element_type=jnp.float32
    )
    phase_angle = slice_phases(shift_index, phase_offset, matrix)
    cosine = jnp.cos(phase_angle)[None, None, :, :, None]
    sine = jnp.sin(phase_angle)[None, None, :, :, None]
    spec_re = spectra[:, :, :, 0]
    spec_im = spectra[:, :, :, 1]
    shifted = jnp.stack(
        [spec_re * cosine - spec_im * sine, spec_re * sine + spec_im * cosine], axis=3
    ).astype(jnp.bfloat16)
    position = lax.axis_index("slc")
    within = jnp.arange(per_device, dtype=jnp.int32)
    classes = (position * per_device + within) % groups
    class_match = (classes[:, None] == jnp.arange(groups, dtype=jnp.int32)[None, :]).astype(
        jnp.int32
    )
    target = jnp.sum(class_match * group_order[None, :], axis=1)
    slot_index = target * spread + within // groups
    onehot = (jnp.arange(slot_count, dtype=jnp.int32)[:, None] == slot_index[None, :]).astype(
        jnp.int32
    )
    source = jnp.sum(onehot * within[None, :], axis=1)
    filled = jnp.sum(onehot, axis=1)
    outgoing = jnp.take(shifted, source, axis=2)
    outgoing = jnp.where(
        filled[None, None, :, None, None, None] > 0, outgoing, jnp.zeros_like(outgoing)
    )
    incoming = lax.all_to_all(outgoing, "slc", split_axis=2, concat_axis=2, tiled=True)
    aliased = jnp.sum(incoming, axis=2, dtype=jnp.float32)
    residual = (aliased - kspace[:, 0].astype(jnp.float32)).astype(jnp.bfloat16)
    partial_value = jnp.einsum(
        "tcpyx,tcyx->py",
        incoming[:, :, :, 0],
        residual[:, :, 1],
        preferred_element_type=jnp.float32,
    )
    partial_value = partial_value - jnp.einsum(
        "tcpyx,tcyx->py",
        incoming[:, :, :, 1],
        residual[:, :, 0],
        preferred_element_type=jnp.float32,
    )
    returned = lax.all_to_all(partial_value, "slc", split_axis=0, concat_axis=0, tiled=True)
    local_grad = jnp.dot(onehot.T.astype(jnp.float32), returned, precision=lax.Precision.HIGHEST)
    summed = lax.psum(local_grad, "coil")
    summed = lax.psum(summed, "vol")
    factor = 1.0 / (
        coil_maps.shape[0] * lax.axis_size("coil") * images.shape[0] * lax.axis_size("vol")
    )
    return summed * factor


def solution(mesh):
    placed = (
        P(("grp", "vol"), "slc", None, None, None),
        P(("grp", "coil"), "slc", None, None, None),
        P(("grp", "vol"), "slc", "coil", None, None, None),
        P("slc"),
        P("slc", None),
        P(),
    )
    return jax.shard_map(
        program, mesh=mesh, in_specs=placed, out_specs=P(("grp", "slc"), None), check_vma=False
    )
```

profile of v0, /device:TPU:0, one launch (start us, length us, event | category | flops | bytes accessed | tf_op | source)
XLA Modules:
  0.0 67.8 jit_solution(9184971657165760032)
XLA Ops:
  0.0 0.0 copy-start
  0.0 0.8 %convert_element_type.10 = f32[8]{0:T(128)S(1)} convert(s32[8]{0:T(128)} %param.12) | non-fusion elementwise | flops 8 | bytes 64 | tf_op jit(solution)/shard_map/convert_element_type | solution.py:29
  0.8 0.8 %fusion.1 = (f32[8,220]{1,0:T(8,128)S(1)}, f32[8,220]{1,0:T(8,128)S(1)}) fusion(f32[8,220]{1,0:T(8,128)} %param.13, f32[220]{0:T(256)S(1)} %add_convert_fusion, f32[8]{0:T(128)S(1)} %convert_element_type.10), kind=kLoop, calls=%fused_computation.3 | loop fusion | flops 5280 | bytes 22032 | tf_op jit(solution)/shard_map/cos | solution.py:322
  1.6 0.8 %copy.13 = f32[16,220]{0,1:T(8,128)} copy(f32[16,220]{1,0:T(8,128)S(1)} %pad_maximum_fusion) | data formatting | bytes 28160 | tf_op jit(solution)/shard_map/concatenate | solution.py:322
  2.4 1.3 %copy.14 = bf16[220,2,2,220]{3,2,1,0:T(2,128)(2,1)S(1)} copy(bf16[220,2,2,220]{3,2,0,1:T(2,128)(2,1)} %bitcast.7) | data formatting | bytes 774400 | tf_op jit(solution)/shard_map/transpose | solution.py:324
  3.7 1.1 %reshape.9.measured_in = bf16[220,880]{1,0:T(8,128)(2,1)} reshape(bf16[220,2,2,220]{3,2,1,0:T(2,128)(2,1)S(1)} %copy.14) | data formatting | bytes 774400 | tf_op jit(solution)/shard_map/reshape | solution.py:324
  4.8 0.0 copy-done
  4.8 1.6 %copy.15.images_ref = bf16[1,8,2,220,220]{4,3,2,1,0:T(8,128)(2,1)} copy(bf16[1,8,2,220,220]{4,2,3,1,0:T(2,128)(2,1)S(1)} %copy-done) | data formatting | bytes 3097600 | tf_op args[0]
  6.4 60.1 %shard_map.91 = f32[8,220]{1,0:T(8,128)} custom-call(s32[4]{0:T(128)} %order_ref.1, f32[220,16]{1,0:T(8,128)} %bitcast.6, bf16[1,8,2,220,220]{4,3,2,1,0:T(8,128)(2,1)} %copy.15.images_ref, bf16[2,8,220,2,220]{4,3,2,1,0:T(2,128)(2,1)} %bitcast.5, bf16[220,880]{1,0:T(8,128)(2,1)} %reshape.9.measured_in, bf16[3,224,220]{2,1,0:T(8,128)(2,1)} %constant.11.clone.first_ref, ...), custom_call_target="tpu_custom_call" | custom-call | tf_op jit(solution)/shard_map/pallas_call | solution.py:330
  66.5 1.3 %copy.17 = f32[8,220]{1,0:T(8,128)} copy(f32[8,220]{1,0:T(8,128)} %shard_map.91) | data formatting | bytes 14080
  (2 shorter events, 0.0 us)
Async XLA Ops:
  0.0 4.8 %copy-start = (bf16[1,8,2,220,220]{4,2,3,1,0:T(2,128)(2,1)S(1)}, bf16[1,8,2,220,220]{4,2,3,1,0:T(2,128)(2,1)}, u32[]{:S(2)}) copy-start(bf16[1,8,2,220,220]{4,2,3,1,0:T(2,128)(2,1)} %param.9) | copy-start | bytes 4646404
where the time goes:
time: 68 us; the launch traced here: 67.8 us
  Pallas kernels  60.1 us (88%)
  local copies, waits for them, and re-layouts  6.03 us (9%)
  other arithmetic  1.61 us (2%)
    pallas_call x1, Pallas kernels, fused(): pl.pallas_call(functools.partial(kernel, sizes), out_shape=jax.ShapeDtype...  60.1 us
    unnamed x4, local copies, waits for them, and re-layouts  2.85 us

commit v1 on v0

--- a/solution.py
+++ b/solution.py
@@ -33,6 +33,8 @@
 
 ROWS = 32
 LAG = 3
+PACE = 2
+AHEAD = 2
 MESH = pl.DeviceIdType.MESH
 F32 = jnp.float32
 BF16 = jnp.bfloat16
@@ -47,41 +49,31 @@
     product = positions[:, None] * positions[None, :] % length
     radians = np.float32(2.0 * math.pi / length) * product.astype(np.float32)
     factor = np.float32(1.0 / math.sqrt(length))
-    cosine = (np.cos(radians) * factor).astype(jnp.bfloat16)
-    sine = (-np.sin(radians) * factor).astype(jnp.bfloat16)
-    return np.asarray(cosine, np.float32), np.asarray(sine, np.float32)
-
-
-def stage_tables(length, coils):
-    cosine, sine = static_tables(length)
-    rows, wide = round_up(length, ROWS), round_up(length, 128)
-    first = np.zeros((3, rows, length), np.float32)
-    first[0, :length], first[1, :length], first[2, :length] = cosine, sine, -sine
-    forward = np.zeros((coils, 2, length, coils * 2 * length), np.float32)
-    back = np.zeros((coils * 2 * length, coils * 2 * wide), np.float32)
-    for coil in range(coils):
-        low = coil * 2 * length
-        mid, top = low + length, low + 2 * length
-        forward[coil, 0, :, low:mid], forward[coil, 0, :, mid:top] = cosine, sine
-        forward[coil, 1, :, low:mid], forward[coil, 1, :, mid:top] = -sine, cosine
-        at = coil * 2 * wide
-        back[low:mid, at : at + length], back[mid:top, at : at + length] = cosine, sine
-        at = at + wide
-        back[low:mid, at : at + length], back[mid:top, at : at + length] = -sine, cosine
-    return first.astype(jnp.bfloat16), forward.astype(jnp.bfloat16), back.astype(jnp.bfloat16)
+    table = np.zeros((2, round_up(length, ROWS), length), np.float32)
+    table[0, :length] = (np.cos(radians) * factor).astype(jnp.bfloat16)
+    table[1, :length] = (-np.sin(radians) * factor).astype(jnp.bfloat16)
+    return table.astype(jnp.bfloat16)
 
 
 def kernel(
     sizes,
+    order_hbm,
+    shift_hbm,
+    offset_hbm,
+    table_hbm,
+    kspace_hbm,
+    images_hbm,
+    maps_hbm,
+    out_ref,
     order_ref,
-    trig_in,
-    images_ref,
+    shift_ref,
+    offset_ref,
+    table_ref,
+    kspace_ref,
+    image_ref,
     maps_ref,
-    measured_in,
-    first_ref,
-    forward_ref,
-    back_ref,
-    out_ref,
+    trig_ref,
+    target,
     turned,
     own,
     to_right,
@@ -89,9 +81,10 @@
     from_left,
     from_right,
     columns,
-    trig_ref,
-    measured_ref,
     shares,
+    small_sems,
+    image_sems,
+    maps_sems,
     right_send,
     left_send,
     left_recv,
@@ -100,22 +93,60 @@
     share_recv,
 ):
     groups, coil_axis, vol_axis = sizes
-    per_device = images_ref.shape[1]
-    length = images_ref.shape[-1]
+    per_device, length = image_ref.shape[0], image_ref.shape[-1]
     coils = maps_ref.shape[0]
-    rows, wide = first_ref.shape[1], turned.shape[-1] // (2 * coils)
+    rows = table_ref.shape[1]
     spread = per_device // groups
     parts = rows // ROWS
     total = groups * parts
     spot = lax.axis_index("slc")
     coil_at, vol_at = lax.axis_index("coil"), lax.axis_index("vol")
     has_left, has_right = spot > 0, spot < groups - 1
+    inner = has_left & has_right
     peers = coil_axis * vol_axis
     mine = coil_at * vol_axis + vol_at
 
     def peer(distance):
         other = lax.rem(mine + distance, peers)
         return {"coil": other // vol_axis, "vol": lax.rem(other, vol_axis)}
+
+    small = [
+        pltpu.make_async_copy(source, target_ref, small_sems.at[which])
+        for which, (source, target_ref) in enumerate(
+            (
+                (table_hbm, table_ref),
+                (offset_hbm, offset_ref),
+                (shift_hbm, shift_ref),
+                (order_hbm, order_ref),
+                (kspace_hbm.at[0, 0], kspace_ref),
+            )
+        )
+    ]
+
+    def slice_of(piece):
+        return piece // spread + lax.rem(piece, spread) * groups
+
+    def image_copy(piece):
+        at = slice_of(piece)
+        return pltpu.make_async_copy(
+            images_hbm.at[0, at], image_ref.at[at], image_sems.at[piece]
+        )
+
+    def maps_copy(piece, coil):
+        at = slice_of(piece)
+        return pltpu.make_async_copy(
+            maps_hbm.at[coil, at], maps_ref.at[coil, at], maps_sems.at[piece, coil]
+        )
+
+    def fetch(piece):
+        image_copy(piece).start()
+        for coil in range(coils):
+            maps_copy(piece, coil).start()
+
+    for copy in small:
+        copy.start()
+    for piece in range(min(AHEAD, per_device)):
+        fetch(piece)
 
     barrier = pltpu.get_barrier_semaphore()
 
@@ -150,64 +181,132 @@
             device_id_type=MESH,
         )
 
-    turned[...] = jnp.zeros_like(turned)
     columns[...] = jnp.zeros_like(columns)
     trig_ref[...] = jnp.zeros_like(trig_ref)
-    measured_ref[...] = jnp.zeros_like(measured_ref)
-    trig_ref[:length] = trig_in[...]
-    measured_ref[:length] = measured_in[...]
+    target[...] = jnp.zeros_like(target)
 
     def dot(left, right):
         return jnp.dot(left, right, preferred_element_type=F32)
 
-    def compute(group):
-        sums = [[None, None] for _ in range(coils)]
+    def planes(ref):
+        pair = jnp.swapaxes(ref[...].astype(F32), 0, 1)
+        return pair[0], pair[1]
+
+    for copy in small:
+        copy.wait()
+
+    row_at = lax.broadcasted_iota(jnp.int32, (per_device, length), 0)
+    line_at = lax.broadcasted_iota(jnp.int32, (per_device, length), 1) - length // 2
+    shift = jnp.zeros((per_device, length), jnp.int32)
+    for at in range(per_device):
+        shift = jnp.where(row_at == at, shift_ref[at], shift)
+    eighths = (shift * line_at) & (MB - 1)
+    angle = 2.0 * math.pi / MB * eighths.astype(F32) + offset_ref[...]
+    trig_ref[0, :length, :per_device] = jnp.cos(angle).T
+    trig_ref[1, :length, :per_device] = jnp.sin(angle).T
+
+    straight, across = table_ref[0, :length], table_ref[1, :length]
+    real_part = jnp.concatenate([straight, -across], axis=1)
+    imaginary_part = jnp.concatenate([across, straight], axis=1)
+    pulled = []
+    for coil in range(coils):
+        seen_re, seen_im = planes(kspace_ref.at[coil])
+        pulled.append(
+            dot(seen_re.astype(BF16), real_part) + dot(seen_im.astype(BF16), imaginary_part)
+        )
+    target[:length] = jnp.concatenate(pulled, axis=1)
+
+    def compute(piece):
+        within, group = slice_of(piece), piece // spread
+        image_copy(piece).wait()
+        for coil in range(coils):
+            maps_copy(piece, coil).wait()
+
+        @pl.when(piece + AHEAD < per_device)
+        def _():
+            fetch(piece + AHEAD)
+
+        lane = lax.broadcasted_iota(jnp.int32, trig_ref.shape[1:], 1)
+        cosine = jnp.sum(jnp.where(lane == within, trig_ref[0], 0.0), axis=1, keepdims=True)
+        sine = jnp.sum(jnp.where(lane == within, trig_ref[1], 0.0), axis=1, keepdims=True)
+        cos_table, sin_table = table_ref[0].astype(F32), table_ref[1].astype(F32)
+        phased_re = cos_table * cosine - sin_table * sine
+        phased_im = cos_table * sine + sin_table * cosine
+        first = jnp.concatenate([phased_re, -phased_im], axis=0).astype(BF16)
+        second = jnp.concatenate([phased_im, phased_re], axis=0).astype(BF16)
+        image_re, image_im = planes(image_ref.at[within])
+        plain, crossed = [], []
+        for coil in range(coils):
+            map_re, map_im = planes(maps_ref.at[coil, within])
+            coil_re = (map_re * image_re - map_im * image_im).astype(BF16)
+            coil_im = (map_re * image_im + map_im * image_re).astype(BF16)
+            plain += [coil_re, coil_im]
+            crossed += [-coil_im, coil_re]
+        both = dot(first, jnp.concatenate(plain, axis=1)) + dot(
+            second, jnp.concatenate(crossed, axis=1)
+        )
+        turned[within] = both[rows:].astype(BF16)
+        span = pl.ds(group * parts, parts)
+        value = both[:rows]
+        if spread == 1:
+            opening = True
+        else:
+            opening = lax.rem(piece, spread) == 0
+        held = jnp.where(order_ref[group] == spot, F32(1.0), F32(0.0))
+
+        def store(fresh):
+            own[span] = fresh.reshape(parts, ROWS, -1)
+
+        if spread == 1:
+            store(value - held * target[...])
+        else:
+
+            @pl.when(opening)
+            def _():
+                store(value - held * target[...])
+
+            @pl.when(jnp.logical_not(opening))
+            def _():
+                store(value + own[span].reshape(rows, -1))
+
+    def launch(group):
+        @pl.when(jnp.logical_not(has_left))
+        def _():
+            def send(chunk, carry):
+                to_right[chunk] = own[chunk].astype(BF16)
+                right_copy(chunk).start()
+                return carry
+
+            lax.fori_loop(group * parts, (group + 1) * parts, send, 0)
+
+        @pl.when(jnp.logical_not(has_right))
+        def _():
+            def send(chunk, carry):
+                to_left[chunk] = own[chunk].astype(BF16)
+                left_copy(chunk).start()
+                return carry
+
+            lax.fori_loop(group * parts, (group + 1) * parts, send, 0)
+
+    skew = 2 * spot - (groups - 1)
+    between = jnp.where(inner, LAG, 0)
+    late_right = between * jnp.maximum(0, skew)
+    late_left = between * jnp.maximum(0, -skew)
+    late = late_right + late_left
+
+    def gradient(chunk):
+        value = own[chunk]
+        value = value + jnp.where(has_left, from_left[chunk].astype(F32), F32(0.0))
+        value = value + jnp.where(has_right, from_right[chunk].astype(F32), F32(0.0))
+        group = chunk // parts
+        at = pl.multiple_of((chunk - group * parts) * ROWS, ROWS)
+        lane = lax.broadcasted_iota(jnp.int32, (ROWS, columns.shape[1]), 1)
+        block = columns[pl.ds(at, ROWS), :]
         for step in range(spread):
             within = group + step * groups
-            image_re = images_ref[0, within, 0].astype(F32)
-            image_im = images_ref[0, within, 1].astype(F32)
-            cosine = trig_ref[:, within : within + 1]
-            sine = trig_ref[:, per_device + within : per_device + within + 1]
-            for coil in range(coils):
-                coil_map = jnp.swapaxes(maps_ref[coil, within].astype(F32), 0, 1)
-                map_re, map_im = coil_map[0], coil_map[1]
-                coil_re = (map_re * image_re - map_im * image_im).astype(BF16)
-                coil_im = (map_re * image_im + map_im * image_re).astype(BF16)
-                part_re = dot(first_ref[0], coil_re) + dot(first_ref[2], coil_im)
-                part_im = dot(first_ref[0], coil_im) + dot(first_ref[1], coil_re)
-                turn_re = part_re * cosine - part_im * sine
-                turn_im = part_re * sine + part_im * cosine
-                at = coil * 2 * wide
-                turned[within, :, at : at + length] = (-turn_im).astype(BF16)
-                turned[within, :, at + wide : at + wide + length] = turn_re.astype(BF16)
-                for which, value in enumerate((turn_re, turn_im)):
-                    before = sums[coil][which]
-                    sums[coil][which] = value if before is None else before + value
-        spectrum = None
-        for coil in range(coils):
-            for which in range(2):
-                term = dot(sums[coil][which].astype(BF16), forward_ref[coil, which])
-                spectrum = term if spectrum is None else spectrum + term
-        held = jnp.where(order_ref[group] == spot, F32(1.0), F32(0.0))
-        spectrum = spectrum - held * measured_ref[...].astype(F32)
-        own[group * parts : (group + 1) * parts] = spectrum.reshape(parts, ROWS, -1)
-
-        @pl.when(jnp.logical_not(has_left))
-        def _():
-            for chunk in range(group * parts, (group + 1) * parts):
-                to_right[chunk] = own[chunk].astype(BF16)
-                right_copy(chunk).start()
-
-        @pl.when(jnp.logical_not(has_right))
-        def _():
-            for chunk in range(group * parts, (group + 1) * parts):
-                to_left[chunk] = own[chunk].astype(BF16)
-                left_copy(chunk).start()
-
-    between = jnp.where(has_left & has_right, LAG, 0)
-    late_right = between * jnp.maximum(0, 2 * spot - (groups - 1))
-    late_left = between * jnp.maximum(0, (groups - 1) - 2 * spot)
-    extra = LAG * (groups - 3)
+            product = value * turned[within, pl.ds(at, ROWS), :].astype(F32)
+            block = jnp.where(lane == within, jnp.sum(product, axis=1, keepdims=True), block)
+        columns[pl.ds(at, ROWS), :] = block
 
     def wave(tick, carry):
         chunk = tick - late_right
@@ -232,43 +331,34 @@
                 to_left[other] = (from_right[other].astype(F32) + own[other]).astype(BF16)
                 left_copy(other).start()
 
+        done = tick - late
+
+        @pl.when(done >= 0)
+        def _():
+            gradient(done)
+
         return carry
 
-    def gradient(group):
-        span = pl.ds(group * parts, parts)
-        value = own[span]
-        value = value + jnp.where(has_left, from_left[span].astype(F32), F32(0.0))
-        value = value + jnp.where(has_right, from_right[span].astype(F32), F32(0.0))
-        value = value.reshape(rows, -1).astype(BF16)
-        pulled = dot(value, back_ref[...])
-        for step in range(spread):
-            within = group + step * groups
-            product = pulled * turned[within].astype(F32)
-            columns[0:rows, within : within + 1] = jnp.sum(product, axis=1, keepdims=True)
-
-    def ticks(group):
-        low = 0 if group == 0 else group * parts + extra
-        high = (group + 1) * parts + extra
-        end_low = group * parts if group == groups - 1 else 0
-        end_high = (group + 1) * parts if group >= groups - 2 else 0
-        inner = has_left & has_right
-        lax.fori_loop(
-            jnp.where(inner, low, end_low), jnp.where(inner, high, end_high), wave, 0
-        )
+    def upto(piece):
+        ready = (piece // spread) * parts
+        wanted = jnp.minimum(jnp.maximum(0, PACE * (piece - spread - 1)), ready)
+        return jnp.where(inner, wanted, 0)
 
     arrivals = has_left.astype(jnp.int32) + has_right.astype(jnp.int32) + (peers - 1)
     pl.semaphore_wait(barrier, arrivals)
-    compute(0)
-    for group in range(1, groups):
-        compute(group)
-        if group < groups - 1:
-            ticks(group - 1)
-    ticks(groups - 2)
-    for group in range(groups - 2):
-        gradient(group)
-    ticks(groups - 1)
-    for group in range(groups - 2, groups):
-        gradient(group)
+
+    def advance(piece, carry):
+        compute(piece)
+
+        @pl.when(lax.rem(piece, spread) == spread - 1)
+        def _():
+            launch(piece // spread)
+
+        lax.fori_loop(upto(piece), upto(piece + 1), wave, 0)
+        return carry
+
+    lax.fori_loop(0, per_device, advance, 0)
+    lax.fori_loop(upto(per_device), total + late, wave, 0)
 
     shares[mine] = columns[...].T[:per_device]
 
@@ -315,34 +405,39 @@
     groups = lax.axis_size("slc")
     sizes = (groups, lax.axis_size("coil"), lax.axis_size("vol"))
     peers = sizes[1] * sizes[2]
-    first, forward, back = stage_tables(length, coils)
-    rows, wide = first.shape[1], back.shape[1] // (2 * coils)
+    table = static_tables(length)
+    rows, wide = table.shape[1], round_up(length, 128)
     width = coils * 2 * length
-    angle = slice_phases(shift_index, phase_offset, length)
-    trig = jnp.concatenate([jnp.cos(angle), jnp.sin(angle)], axis=0)
-    trig = trig.T
-    measured = jnp.moveaxis(kspace[0, 0], 2, 0).reshape(length, width)
     chunks = groups * rows // ROWS
-    vmem = pl.BlockSpec(memory_space=pltpu.VMEM)
-    smem = pl.BlockSpec(memory_space=pltpu.SMEM)
+    anywhere = pl.BlockSpec(memory_space=pl.ANY)
     block = pltpu.VMEM((chunks, ROWS, width), BF16)
     side = pltpu.SemaphoreType.DMA((chunks,))
     return pl.pallas_call(
         functools.partial(kernel, sizes),
         out_shape=jax.ShapeDtypeStruct((per_device, length), F32),
-        in_specs=[smem] + [vmem] * 7,
-        out_specs=vmem,
+        in_specs=[anywhere] * 7,
+        out_specs=pl.BlockSpec(memory_space=pltpu.VMEM),
         scratch_shapes=[
-            pltpu.VMEM((per_device, rows, coils * 2 * wide), BF16),
+            pltpu.SMEM(group_order.shape, jnp.int32),
+            pltpu.SMEM(shift_index.shape, jnp.int32),
+            pltpu.VMEM((per_device, length), F32),
+            pltpu.VMEM(table.shape, BF16),
+            pltpu.VMEM((coils, length, 2, length), BF16),
+            pltpu.VMEM((per_device, length, 2, length), BF16),
+            pltpu.VMEM((coils, per_device, length, 2, length), BF16),
+            pltpu.VMEM((2, rows, 128), F32),
+            pltpu.VMEM((rows, width), F32),
+            pltpu.VMEM((per_device, rows, width), BF16),
             pltpu.VMEM((chunks, ROWS, width), F32),
             block,
             block,
             block,
             block,
             pltpu.VMEM((wide, 128), F32),
-            pltpu.VMEM((rows, 2 * per_device), F32),
-            pltpu.VMEM((rows, width), BF16),
             pltpu.VMEM((peers, per_device, wide), F32),
+            pltpu.SemaphoreType.DMA((5,)),
+            pltpu.SemaphoreType.DMA((per_device,)),
+            pltpu.SemaphoreType.DMA((per_device, coils)),
             side,
             side,
             side,
@@ -355,13 +450,12 @@
         ),
     )(
         group_order,
-        trig,
-        images,
+        shift_index,
+        phase_offset,
+        jnp.asarray(table),
+        jnp.swapaxes(kspace, 3, 4),
+        jnp.swapaxes(images, 2, 3),
         jnp.swapaxes(coil_maps, 2, 3),
-        measured,
-        jnp.asarray(first),
-        jnp.asarray(forward),
-        jnp.asarray(back),
     )
 
 

time: 68 us -> 58.5 us (0.86)
  local copies, waits for them, and re-layouts: 6.03 us -> 1.3 us
  Pallas kernels: 60.1 us -> 57 us
  other arithmetic: 1.61 us -> 0 us
    pallas_call x1, Pallas kernels: 60.1 us -> 57 us  [fused(): pl.pallas_call(functools.partial(kernel, sizes), out_shape=jax.ShapeDtype...]
    unnamed x4 -> x1, local copies, waits for them, and re-layouts: 2.85 us -> 1.3 us
    transpose x1 -> x0, local copies, waits for them, and re-layouts: 1.33 us -> none  [fused(): measured = jnp.moveaxis(kspace[0, 0], 2, 0).reshape(length, width)]
    reshape x1 -> x0, local copies, waits for them, and re-layouts: 1.1 us -> none  [fused(): measured = jnp.moveaxis(kspace[0, 0], 2, 0).reshape(length, width)]
    cos x1 -> x0, other arithmetic: 0.81 us -> none  [fused(): trig = jnp.concatenate([jnp.cos(angle), jnp.sin(angle)], axis=0)]
    convert_element_type x2 -> x0, other arithmetic: 0.79 us -> none  [the longest x1 0.79 us: slice_phases(): shift_index.astype(jnp.float32)[:, None] * lines[None, :]]
    concatenate x1 -> x0, local copies, waits for them, and re-layouts: 0.75 us -> none  [fused(): trig = jnp.concatenate([jnp.cos(angle), jnp.sin(angle)], axis=0)]
where the time goes in v1:
time: 58.5 us; the launch traced here: 58.3 us
  Pallas kernels  57 us (97%)
  local copies, waits for them, and re-layouts  1.3 us (2%)
    pallas_call x1, Pallas kernels, fused(): pl.pallas_call(functools.partial(kernel, sizes), out_shape=jax.ShapeDtype...  57 us
    unnamed x1, local copies, waits for them, and re-layouts  1.3 us

profile of v1, /device:TPU:0, one launch (start us, length us, event | category | flops | bytes accessed | tf_op | source)
XLA Modules:
  0.0 58.3 jit_solution(10281585409008648963)
XLA Ops:
  0.0 57.0 %shard_map.73 = f32[8,220]{1,0:T(8,128)} custom-call(s32[4]{0:T(128)} %order_hbm.1, s32[8]{0:T(128)} %shift_hbm.1, f32[8,220]{1,0:T(8,128)} %offset_hbm.1, bf16[2,224,220]{2,1,0:T(8,128)(2,1)} %constant.2.clone.table_hbm, bf16[1,1,2,220,2,220]{5,4,3,2,1,0:T(2,128)(2,1)} %bitcast.5, bf16[1,8,220,2,220]{4,3,2,1,0:T(2,128)(2,1)} %bitcast.4, ...), custom_call_target="tpu_custom_call" | custom-call | tf_op jit(solution)/shard_map/pallas_call | solution.py:415
  57.0 1.3 %copy.9 = f32[8,220]{1,0:T(8,128)} copy(f32[8,220]{1,0:T(8,128)} %shard_map.73) | data formatting | bytes 14080

commit v2 on v1

--- a/solution.py
+++ b/solution.py
@@ -32,7 +32,7 @@
 
 
 ROWS = 32
-LAG = 3
+LAG = 4
 PACE = 2
 AHEAD = 2
 MESH = pl.DeviceIdType.MESH
@@ -49,9 +49,12 @@
     product = positions[:, None] * positions[None, :] % length
     radians = np.float32(2.0 * math.pi / length) * product.astype(np.float32)
     factor = np.float32(1.0 / math.sqrt(length))
-    table = np.zeros((2, round_up(length, ROWS), length), np.float32)
-    table[0, :length] = (np.cos(radians) * factor).astype(jnp.bfloat16)
-    table[1, :length] = (-np.sin(radians) * factor).astype(jnp.bfloat16)
+    cosine = (np.cos(radians) * factor).astype(jnp.bfloat16)
+    sine = (-np.sin(radians) * factor).astype(jnp.bfloat16)
+    deep = round_up(length, 128)
+    table = np.zeros((2, round_up(length, ROWS), 2 * deep), np.float32)
+    table[0, :length, :length], table[0, :length, deep : deep + length] = cosine, sine
+    table[1, :length, :length], table[1, :length, deep : deep + length] = -sine, cosine
     return table.astype(jnp.bfloat16)
 
 
@@ -74,6 +77,11 @@
     maps_ref,
     trig_ref,
     target,
+    phased,
+    crossing,
+    stacked,
+    seen,
+    stage,
     turned,
     own,
     to_right,
@@ -94,8 +102,9 @@
 ):
     groups, coil_axis, vol_axis = sizes
     per_device, length = image_ref.shape[0], image_ref.shape[-1]
+    flat = (2 * length, length)
     coils = maps_ref.shape[0]
-    rows = table_ref.shape[1]
+    rows, deep = table_ref.shape[1], table_ref.shape[2] // 2
     spread = per_device // groups
     parts = rows // ROWS
     total = groups * parts
@@ -118,10 +127,15 @@
                 (offset_hbm, offset_ref),
                 (shift_hbm, shift_ref),
                 (order_hbm, order_ref),
-                (kspace_hbm.at[0, 0], kspace_ref),
             )
         )
     ]
+    small += [
+        pltpu.make_async_copy(
+            kspace_hbm.at[0, 0, coil].reshape(flat), kspace_ref.at[coil], small_sems.at[4 + coil]
+        )
+        for coil in range(coils)
+    ]
 
     def slice_of(piece):
         return piece // spread + lax.rem(piece, spread) * groups
@@ -129,13 +143,13 @@
     def image_copy(piece):
         at = slice_of(piece)
         return pltpu.make_async_copy(
-            images_hbm.at[0, at], image_ref.at[at], image_sems.at[piece]
+            images_hbm.at[0, at].reshape(flat), image_ref.at[at], image_sems.at[piece]
         )
 
     def maps_copy(piece, coil):
         at = slice_of(piece)
         return pltpu.make_async_copy(
-            maps_hbm.at[coil, at], maps_ref.at[coil, at], maps_sems.at[piece, coil]
+            maps_hbm.at[coil, at].reshape(flat), maps_ref.at[coil, at], maps_sems.at[piece, coil]
         )
 
     def fetch(piece):
@@ -188,9 +202,30 @@
     def dot(left, right):
         return jnp.dot(left, right, preferred_element_type=F32)
 
-    def planes(ref):
-        pair = jnp.swapaxes(ref[...].astype(F32), 0, 1)
-        return pair[0], pair[1]
+    blocks = [(low, min(low + ROWS, length)) for low in range(0, length, ROWS)]
+
+    lanes = [(low, min(low + 128, length)) for low in range(0, length, 128)]
+
+    def unfold(slot, ref):
+        for tile, (left, right) in enumerate(lanes):
+            stage[slot, tile, :, : right - left] = ref[:, left:right].astype(F32)
+
+    def planes(slot, low, high):
+        pair = []
+        for part in range(2):
+            pieces = []
+            for tile, (left, right) in enumerate(lanes):
+                every = pl.ds(2 * low + part, high - low, stride=2)
+                pieces.append(stage[slot, tile, every, :][:, : right - left])
+            pair.append(jnp.concatenate(pieces, axis=1))
+        return pair
+
+    def side_by_side(parts_of):
+        filled = []
+        for part in parts_of:
+            filled.append(part)
+            filled.append(jnp.zeros((part.shape[0], rows - length), part.dtype))
+        return jnp.concatenate(filled, axis=1)
 
     for copy in small:
         copy.wait()
@@ -205,19 +240,28 @@
     trig_ref[0, :length, :per_device] = jnp.cos(angle).T
     trig_ref[1, :length, :per_device] = jnp.sin(angle).T
 
-    straight, across = table_ref[0, :length], table_ref[1, :length]
-    real_part = jnp.concatenate([straight, -across], axis=1)
-    imaginary_part = jnp.concatenate([across, straight], axis=1)
+    straight = table_ref[0, :length, :length]
+    across = table_ref[0, :length, deep : deep + length]
     pulled = []
     for coil in range(coils):
-        seen_re, seen_im = planes(kspace_ref.at[coil])
-        pulled.append(
-            dot(seen_re.astype(BF16), real_part) + dot(seen_im.astype(BF16), imaginary_part)
-        )
-    target[:length] = jnp.concatenate(pulled, axis=1)
+        unfold(coil, kspace_ref.at[coil])
+        for low, high in blocks:
+            seen_re, seen_im = planes(coil, low, high)
+            seen[0, low:high] = seen_re.astype(BF16)
+            seen[1, low:high] = seen_im.astype(BF16)
+        seen_re, seen_im = seen[0], seen[1]
+        pulled.append(dot(seen_re, straight) + dot(seen_im, across))
+        pulled.append(dot(seen_im, straight) - dot(seen_re, across))
+    target[:length] = side_by_side(pulled)
+
+    def phases(within):
+        lane = lax.broadcasted_iota(jnp.int32, trig_ref.shape[1:], 1)
+        cosine = jnp.sum(jnp.where(lane == within, trig_ref[0], 0.0), axis=1, keepdims=True)
+        sine = jnp.sum(jnp.where(lane == within, trig_ref[1], 0.0), axis=1, keepdims=True)
+        return cosine, sine
 
     def compute(piece):
-        within, group = slice_of(piece), piece // spread
+        within, step = slice_of(piece), lax.rem(piece, spread)
         image_copy(piece).wait()
         for coil in range(coils):
             maps_copy(piece, coil).wait()
@@ -226,48 +270,48 @@
         def _():
             fetch(piece + AHEAD)
 
-        lane = lax.broadcasted_iota(jnp.int32, trig_ref.shape[1:], 1)
-        cosine = jnp.sum(jnp.where(lane == within, trig_ref[0], 0.0), axis=1, keepdims=True)
-        sine = jnp.sum(jnp.where(lane == within, trig_ref[1], 0.0), axis=1, keepdims=True)
-        cos_table, sin_table = table_ref[0].astype(F32), table_ref[1].astype(F32)
-        phased_re = cos_table * cosine - sin_table * sine
-        phased_im = cos_table * sine + sin_table * cosine
-        first = jnp.concatenate([phased_re, -phased_im], axis=0).astype(BF16)
-        second = jnp.concatenate([phased_im, phased_re], axis=0).astype(BF16)
-        image_re, image_im = planes(image_ref.at[within])
-        plain, crossed = [], []
+        cosine, sine = phases(within)
+        for low in range(0, rows, ROWS):
+            span = slice(low, low + ROWS)
+            turn = table_ref[0, span].astype(F32) * cosine[span]
+            turn = turn + table_ref[1, span].astype(F32) * sine[span]
+            phased[step, span] = turn.astype(BF16)
+        edge = length // 16 * 16
+        for half in range(2):
+            stacked[piece, half * deep + edge : (half + 1) * deep] = jnp.zeros(
+                (deep - edge, stacked.shape[2]), BF16
+            )
+        unfold(coils, image_ref.at[within])
         for coil in range(coils):
-            map_re, map_im = planes(maps_ref.at[coil, within])
-            coil_re = (map_re * image_re - map_im * image_im).astype(BF16)
-            coil_im = (map_re * image_im + map_im * image_re).astype(BF16)
-            plain += [coil_re, coil_im]
-            crossed += [-coil_im, coil_re]
-        both = dot(first, jnp.concatenate(plain, axis=1)) + dot(
-            second, jnp.concatenate(crossed, axis=1)
-        )
-        turned[within] = both[rows:].astype(BF16)
-        span = pl.ds(group * parts, parts)
-        value = both[:rows]
-        if spread == 1:
-            opening = True
-        else:
-            opening = lax.rem(piece, spread) == 0
+            unfold(coil, maps_ref.at[coil, within])
+        for low, high in blocks:
+            image_re, image_im = planes(coils, low, high)
+            plain, crossed = [], []
+            for coil in range(coils):
+                map_re, map_im = planes(coil, low, high)
+                coil_re = (map_re * image_re - map_im * image_im).astype(BF16)
+                coil_im = (map_re * image_im + map_im * image_re).astype(BF16)
+                plain += [coil_re, coil_im]
+                crossed += [-coil_im, coil_re]
+            stacked[piece, low:high] = side_by_side(plain)
+            stacked[piece, deep + low : deep + high] = side_by_side(crossed)
+
+    def combine(group):
+        left = jnp.concatenate([phased[step] for step in range(spread)], axis=1)
+        right = stacked[pl.ds(group * spread, spread)].reshape(spread * 2 * deep, -1)
         held = jnp.where(order_ref[group] == spot, F32(1.0), F32(0.0))
-
-        def store(fresh):
-            own[span] = fresh.reshape(parts, ROWS, -1)
-
-        if spread == 1:
-            store(value - held * target[...])
-        else:
-
-            @pl.when(opening)
-            def _():
-                store(value - held * target[...])
-
-            @pl.when(jnp.logical_not(opening))
-            def _():
-                store(value + own[span].reshape(rows, -1))
+        value = dot(left, right) - held * target[...]
+        own[pl.ds(group * parts, parts)] = value.reshape(parts, ROWS, -1)
+
+    def rotate(piece):
+        within = slice_of(piece)
+        cosine, sine = phases(within)
+        for low in range(0, rows, ROWS):
+            span = slice(low, low + ROWS)
+            turn = table_ref[1, span].astype(F32) * cosine[span]
+            turn = turn - table_ref[0, span].astype(F32) * sine[span]
+            crossing[span] = turn.astype(BF16)
+        turned[within] = dot(crossing[...], stacked[piece]).astype(BF16)
 
     def launch(group):
         @pl.when(jnp.logical_not(has_left))
@@ -340,7 +384,7 @@
         return carry
 
     def upto(piece):
-        ready = (piece // spread) * parts
+        ready = (jnp.maximum(piece - 1, 0) // spread) * parts
         wanted = jnp.minimum(jnp.maximum(0, PACE * (piece - spread - 1)), ready)
         return jnp.where(inner, wanted, 0)
 
@@ -352,12 +396,19 @@
 
         @pl.when(lax.rem(piece, spread) == spread - 1)
         def _():
+            combine(piece // spread)
             launch(piece // spread)
+
+        @pl.when(piece >= spread - 1)
+        def _():
+            rotate(piece - (spread - 1))
 
         lax.fori_loop(upto(piece), upto(piece + 1), wave, 0)
         return carry
 
     lax.fori_loop(0, per_device, advance, 0)
+    for piece in range(per_device - spread + 1, per_device):
+        rotate(piece)
     lax.fori_loop(upto(per_device), total + late, wave, 0)
 
     shares[mine] = columns[...].T[:per_device]
@@ -396,7 +447,7 @@
     result = shares[0]
     for other in range(1, peers):
         result = result + shares[other]
-    out_ref[...] = result[:, :length] * (1.0 / (coils * peers))
+    out_ref[...] = result[:, :length]
 
 
 def fused(images, coil_maps, kspace, shift_index, phase_offset, group_order):
@@ -407,12 +458,13 @@
     peers = sizes[1] * sizes[2]
     table = static_tables(length)
     rows, wide = table.shape[1], round_up(length, 128)
-    width = coils * 2 * length
+    width, deep = coils * 2 * rows, table.shape[2] // 2
+    spread = per_device // groups
     chunks = groups * rows // ROWS
     anywhere = pl.BlockSpec(memory_space=pl.ANY)
     block = pltpu.VMEM((chunks, ROWS, width), BF16)
     side = pltpu.SemaphoreType.DMA((chunks,))
-    return pl.pallas_call(
+    summed = pl.pallas_call(
         functools.partial(kernel, sizes),
         out_shape=jax.ShapeDtypeStruct((per_device, length), F32),
         in_specs=[anywhere] * 7,
@@ -422,11 +474,16 @@
             pltpu.SMEM(shift_index.shape, jnp.int32),
             pltpu.VMEM((per_device, length), F32),
             pltpu.VMEM(table.shape, BF16),
-            pltpu.VMEM((coils, length, 2, length), BF16),
-            pltpu.VMEM((per_device, length, 2, length), BF16),
-            pltpu.VMEM((coils, per_device, length, 2, length), BF16),
+            pltpu.VMEM((coils, 2 * length, length), BF16),
+            pltpu.VMEM((per_device, 2 * length, length), BF16),
+            pltpu.VMEM((coils, per_device, 2 * length, length), BF16),
             pltpu.VMEM((2, rows, 128), F32),
             pltpu.VMEM((rows, width), F32),
+            pltpu.VMEM((spread, rows, 2 * deep), BF16),
+            pltpu.VMEM((rows, 2 * deep), BF16),
+            pltpu.VMEM((per_device, 2 * deep, width), BF16),
+            pltpu.VMEM((2, length, length), BF16),
+            pltpu.VMEM((coils + 1, wide // 128, 2 * length, 128), F32),
             pltpu.VMEM((per_device, rows, width), BF16),
             pltpu.VMEM((chunks, ROWS, width), F32),
             block,
@@ -435,7 +492,7 @@
             block,
             pltpu.VMEM((wide, 128), F32),
             pltpu.VMEM((peers, per_device, wide), F32),
-            pltpu.SemaphoreType.DMA((5,)),
+            pltpu.SemaphoreType.DMA((4 + coils,)),
             pltpu.SemaphoreType.DMA((per_device,)),
             pltpu.SemaphoreType.DMA((per_device, coils)),
             side,
@@ -457,6 +514,7 @@
         jnp.swapaxes(images, 2, 3),
         jnp.swapaxes(coil_maps, 2, 3),
     )
+    return summed * (1.0 / (coils * peers))
 
 
 def program(images, coil_maps, kspace, shift_index, phase_offset, group_order):

time: 58.5 us -> 56.7 us (0.969)
  Pallas kernels: 57 us -> 55.2 us
  other arithmetic: 0 us -> 1.3 us
  local copies, waits for them, and re-layouts: 1.3 us -> 0 us
    pallas_call x1, Pallas kernels: 57 us -> 55.2 us  [fused(): pl.pallas_call(functools.partial(kernel, sizes), out_shape=jax.ShapeDtype...]
    mul x0 -> x1, other arithmetic: none -> 1.3 us  [fused(): return summed * (1.0 / (coils * peers))]
    unnamed x1 -> x0, local copies, waits for them, and re-layouts: 1.3 us -> none
where the time goes in v2:
time: 56.7 us; the launch traced here: 56.5 us
  Pallas kernels  55.2 us (97%)
  other arithmetic  1.3 us (2%)
    pallas_call x1, Pallas kernels, fused(): pl.pallas_call(functools.partial(kernel, sizes), out_shape=jax.ShapeDtype...  55.2 us
    mul x1, other arithmetic, fused(): return summed * (1.0 / (coils * peers))  1.3 us

profile of v2, /device:TPU:0, one launch (start us, length us, event | category | flops | bytes accessed | tf_op | source)
XLA Modules:
  0.0 56.5 jit_solution(10307137211945809268)
XLA Ops:
  0.0 55.2 %shard_map.73 = f32[8,220]{1,0:T(8,128)} custom-call(s32[4]{0:T(128)} %order_hbm.1, s32[8]{0:T(128)} %shift_hbm.1, f32[8,220]{1,0:T(8,128)} %offset_hbm.1, bf16[2,224,512]{2,1,0:T(8,128)(2,1)} %constant.4.clone.table_hbm, bf16[1,1,2,220,2,220]{5,4,3,2,1,0:T(2,128)(2,1)} %bitcast.5, bf16[1,8,220,2,220]{4,3,2,1,0:T(2,128)(2,1)} %bitcast.4, ...), custom_call_target="tpu_custom_call" | custom-call | tf_op jit(solution)/shard_map/pallas_call | solution.py:467
  55.2 1.3 %broadcast_multiply_fusion = f32[8,220]{1,0:T(8,128)} fusion(f32[8,220]{1,0:T(8,128)} %shard_map.73), kind=kLoop, calls=%fused_computation | loop fusion | flops 1760 | bytes 14080 | tf_op jit(solution)/shard_map/mul | solution.py:517
